TPU v7x, 32 devices: a whole 2x2x4 slice. The times are simulated.
32 devices in a mesh: row: 8 (over z, x), col: 4 (over y, core).
Axes of the slice: x: 2, y: 2, z: 4, core: 2. Of those that a mesh axis runs over, the one named last changes fastest.
Arguments:
- pixels: bfloat16 [512, 512, 384], P('row', 'col'), may hold values from -40 to 40, as said below
- start: float32 [384, 64], replicated, may hold values from -0.3125 to 0.3125
Outputs:
- mean: float32 [384], replicated
- projector: float32 [384, 384], replicated
- scores: float32 [64, 512, 512], P(None, 'row', 'col')
Inputs may be any that keep to these rules, and one draw needn't show every extreme that they name: `pixels`: Real-valued features.
All inputs are finite; a program needn't handle non-finite values.
Results may differ from a plain program's by a relative error of at most 0.0029.
Values may be sent and summed in bfloat16 or wider, within the bound.
No kernel may reach another device: no remote copies, remote signals or barrier semaphores. Data moves between devices by JAX's collectives and lax.ppermute only.
A program may use at most 64 MiB of HBM per device.

v0:
```python
import jax
import jax.numpy as jnp
from jax import lax
from jax.sharding import PartitionSpec as P

ITERS = 4
GAUSS = (0.0625, 0.25, 0.375, 0.25, 0.0625)


def padded_2(shard, sides, width):
    for axis, dim in sides:
        size, length = (lax.axis_size(axis), shard.shape[dim])
        up = [(i, (i + 1) % size) for i in range(size - 1)]
        down = [(j, i) for i, j in up]
        last = lax.slice_in_dim(shard, length - width, length, axis=dim)
        first = lax.slice_in_dim(shard, 0, width, axis=dim)
        before = lax.ppermute(last, axis, up)
        after = lax.ppermute(first, axis, down)
        shard = jnp.concatenate([before, shard, after], axis=dim)
    return shard


def edge_weight(first, count, total):
    position = first + jnp.arange(count, dtype=jnp.int32)
    weight = jnp.zeros((count,), jnp.float32)
    for offset in range(5):
        inside = (position + offset - 2 >= 0) & (position + offset - 2 < total)
        weight = weight + GAUSS[offset] * inside.astype(jnp.float32)
    return weight


def along_rows(padded, count):
    total = GAUSS[0] * padded[0:count].astype(jnp.float32)
    for offset in range(1, 5):
        total = total + GAUSS[offset] * padded[offset : offset + count].astype(jnp.float32)
    return total


def along_cols(padded, count):
    total = GAUSS[0] * padded[:, 0:count]
    for offset in range(1, 5):
        total = total + GAUSS[offset] * padded[:, offset : offset + count]
    return total


def orthonormal(product):
    inner = jnp.dot(product.T, product, precision=lax.Precision.HIGHEST)
    lower_factor = jnp.linalg.cholesky(inner)
    return lax.linalg.triangular_solve(
        lower_factor, product, left_side=False, lower=True, transpose_a=True
    )


def local(pixels, start):
    tile_rows, tile_cols, feat = pixels.shape
    rows_total = tile_rows * lax.axis_size("row")
    cols_total = tile_cols * lax.axis_size("col")
    padded = padded_2(pixels, (("row", 0), ("col", 1)), 2)
    blurred = along_cols(along_rows(padded, tile_rows), tile_cols)
    row_weight = edge_weight(lax.axis_index("row") * tile_rows, tile_rows, rows_total)
    col_weight = edge_weight(lax.axis_index("col") * tile_cols, tile_cols, cols_total)
    weight = row_weight[:, None, None] * col_weight[None, :, None]
    smoothed = (blurred / weight).astype(jnp.bfloat16)
    flat = smoothed.reshape(tile_rows * tile_cols, feat)
    gram_local = lax.dot_general(
        flat, flat, (((0,), (0,)), ((), ())), preferred_element_type=jnp.float32
    )
    sums_local = jnp.sum(flat, axis=0, dtype=jnp.float32)
    count = float(rows_total * cols_total)
    basis = start
    gram, sums = lax.psum((gram_local, sums_local), ("row", "col"))
    mean = sums / count
    cov = gram / count - mean[:, None] * mean[None, :]
    for step in range(ITERS):
        basis = orthonormal(jnp.dot(cov, basis, precision=lax.Precision.HIGHEST))
    projector = jnp.dot(basis, basis.T, precision=lax.Precision.HIGHEST)
    basis_b = basis.astype(jnp.bfloat16)
    shift = jnp.dot(mean, basis_b.astype(jnp.float32), precision=lax.Precision.HIGHEST)
    scores = lax.dot_general(
        basis_b, flat, (((0,), (1,)), ((), ())), preferred_element_type=jnp.float32
    )
    scores = scores - shift[:, None]
    return (mean, projector, scores.reshape(basis.shape[1], tile_rows, tile_cols))


def solution(mesh):
    in_specs = (P("row", "col", None), P())
    out_specs = (P(), P(), P(None, "row", "col"))
    return jax.shard_map(local, mesh=mesh, in_specs=in_specs, out_specs=out_specs, check_vma=False)
```

profile of v0, /device:TPU:0, one launch (start us, length us, event | category | flops | bytes accessed | tf_op | source)
XLA Modules:
  0.0 266.5 jit_solution(16941923063009096975)
XLA Ops:
  8.3 4.9 %collective-permute-start = (bf16[2,128,384]{2,1,0:T(8,128)(2,1)S(1)}, bf16[2,128,384]{2,1,0:T(8,128)(2,1)S(1)}, u32[]{:S(2)}, u32[]{:S(2)}) collective-permute-start(bf16[2,128,384]{2,1,0:T(8,128)(2,1)S(1)} %get-tuple-element.10), channel_id=1, source_target_pairs={{0,4},{4,8},{8,12},{12,16},{16,20},{20,24},{24,28},{1,5},{5,9},{9,... | collective-permute-start | bytes 589832 | tf_op jit(solution)/shard_map/ppermute | solution.py:17
  14.5 2.9 %collective-permute-done = bf16[2,128,384]{2,1,0:T(8,128)(2,1)S(1)} collective-permute-done((bf16[2,128,384]{2,1,0:T(8,128)(2,1)S(1)}, bf16[2,128,384]{2,1,0:T(8,128)(2,1)S(1)}, u32[]{:S(2)}, u32[]{:S(2)}) %collective-permute-start) | collective-permute-done | bytes 196640 | tf_op jit(solution)/shard_map/ppermute | solution.py:17
  17.4 4.6 %constant_dynamic-update-slice_fusion.1 = bf16[68,128,384]{2,1,0:T(8,128)(2,1)S(1)} fusion(bf16[68,128,384]{2,1,0:T(8,128)(2,1)S(1)} %constant_dynamic-update-slice_fusion.2, bf16[64,128,384]{2,1,0:T(8,128)(2,1)} %param.5), kind=kLoop, calls=%fused_computation.56 | loop fusion | bytes 12582912
  24.9 3.6 %collective-permute-done.3 = bf16[68,2,384]{2,1,0:T(2,128)(2,1)S(1)} collective-permute-done((bf16[68,2,384]{2,1,0:T(2,128)(2,1)S(1)}, bf16[68,2,384]{2,1,0:T(2,128)(2,1)S(1)}, u32[]{:S(2)}, u32[]{:S(2)}) %collective-permute-start.3) | collective-permute-done | bytes 104480 | tf_op jit(solution)/shard_map/ppermute | solution.py:18
  28.5 3.6 %pad_maximum_fusion = bf16[68,132,384]{2,1,0:T(8,128)(2,1)S(1)} fusion(bf16[68,2,384]{2,1,0:T(2,128)(2,1)S(1)} %collective-permute-done.3, bf16[68,128,384]{2,1,0:T(8,128)(2,1)S(1)} %constant_dynamic-update-slice_fusion, bf16[68,2,384]{2,1,0:T(2,128)(2,1)S(1)} %collective-permute-done.2), kind=kLoop, calls=%fused_computation.14 | loop fusion | flops 20680704 | bytes 13787136 | tf_op jit(solution)/shard_map/concatenate | solution.py:19
  32.1 6.2 %multiply_add_fusion = f32[64,132,384]{2,1,0:T(8,128)S(1)} fusion(bf16[68,132,384]{2,1,0:T(8,128)(2,1)S(1)} %pad_maximum_fusion), kind=kLoop, calls=%fused_computation | loop fusion | flops 45416448 | bytes 45416448 | tf_op jit(solution)/shard_map/add | solution.py:35
  38.3 9.7 %convert_reduce_fusion = (f32[384]{0:T(512)S(1)}, bf16[64,128,384]{2,1,0:T(8,128)(2,1)}) fusion(f32[64,128]{1,0:T(8,128)S(1)} %broadcast_multiply_fusion, f32[64,132,384]{2,1,0:T(8,128)S(1)} %multiply_add_fusion), kind=kLoop, calls=%fused_computation.11 | loop fusion | flops 40894080 | bytes 69240320 | tf_op jit(solution)/shard_map/reduce_sum | solution.py:68
  48.1 8.8 %convolution_bitcast_fusion = f32[384,384]{1,0:T(8,128)} fusion(bf16[64,128,384]{2,1,0:T(8,128)(2,1)} %get-tuple-element.6), kind=kOutput, calls=%fused_computation.16 | convolution fusion | flops 2415919104 | bytes 6881280 | tf_op jit(solution)/shard_map/dot_general | solution.py:65
  56.9 47.5 %psum.14 = f32[384]{0:T(512)S(1)} all-reduce(f32[384]{0:T(512)S(1)} %get-tuple-element.5), channel_id=1, replica_groups=mesh['row'=8,'col'=4] {'row','col'}, use_global_device_ids=true, to_apply=%region_1.0 | all-reduce | flops 384 | bytes 3072 | tf_op jit(solution)/shard_map/psum | solution.py:71
  104.5 88.2 %all-reduce.2.cloned.1.call-done = f32[384,384]{1,0:T(8,128)} async-done(((f32[384,384]{1,0:T(8,128)}), f32[384,384]{1,0:T(8,128)}) %all-reduce.2.cloned.1.call-update) | async-done | bytes 589840 | tf_op jit(solution)/shard_map/psum | solution.py:71
  192.7 1.9 fusion.38
  195.0 5.8 %cholesky.74 = f32[64,64]{1,0:T(8,128)S(1)} custom-call(f32[64,64]{1,0:T(8,128)S(1)} %fusion.18), custom_call_target="Cholesky" | custom-call | tf_op jit(solution)/shard_map/jit(cholesky)/cholesky | solution.py:48
  202.2 4.9 %custom-call.8 = f32[1,64,64]{1,2,0:T(8,128)S(1)} custom-call(f32[1,64,64]{2,1,0:T(8,128)S(1)} %fusion.7), custom_call_target="InvertDiagBlocksLowerTriangular" | custom-call | tf_op jit(solution)/shard_map/triangular_solve/custom-call.0 | solution.py:49
  207.4 1.9 fusion.37
  209.7 5.8 %cholesky.85 = f32[64,64]{1,0:T(8,128)S(1)} custom-call(f32[64,64]{1,0:T(8,128)S(1)} %fusion.16), custom_call_target="Cholesky" | custom-call | tf_op jit(solution)/shard_map/jit(cholesky)/cholesky | solution.py:48
  216.9 4.9 %custom-call.9 = f32[1,64,64]{1,2,0:T(8,128)S(1)} custom-call(f32[1,64,64]{2,1,0:T(8,128)S(1)} %fusion.8), custom_call_target="InvertDiagBlocksLowerTriangular" | custom-call | tf_op jit(solution)/shard_map/triangular_solve/custom-call.0 | solution.py:49
  222.1 1.9 fusion.36
  224.4 5.8 %cholesky.96 = f32[64,64]{1,0:T(8,128)S(1)} custom-call(f32[64,64]{1,0:T(8,128)S(1)} %fusion.14), custom_call_target="Cholesky" | custom-call | tf_op jit(solution)/shard_map/jit(cholesky)/cholesky | solution.py:48
  231.6 4.9 %custom-call.10 = f32[1,64,64]{1,2,0:T(8,128)S(1)} custom-call(f32[1,64,64]{2,1,0:T(8,128)S(1)} %fusion.9), custom_call_target="InvertDiagBlocksLowerTriangular" | custom-call | tf_op jit(solution)/shard_map/triangular_solve/custom-call.0 | solution.py:49
  236.8 1.9 fusion.35
  239.1 5.8 %cholesky.107 = f32[64,64]{1,0:T(8,128)S(1)} custom-call(f32[64,64]{1,0:T(8,128)S(1)} %fusion.12), custom_call_target="Cholesky" | custom-call | tf_op jit(solution)/shard_map/jit(cholesky)/cholesky | solution.py:48
  246.2 4.9 %custom-call.11 = f32[1,64,64]{1,2,0:T(8,128)S(1)} custom-call(f32[1,64,64]{2,1,0:T(8,128)S(1)} %fusion.10), custom_call_target="InvertDiagBlocksLowerTriangular" | custom-call | tf_op jit(solution)/shard_map/triangular_solve/custom-call.0 | solution.py:49
  253.0 4.9 %fusion.6 = f32[8,8,64,128]{3,1,2,0:T(8,128)S(1)} fusion(bf16[8192,384]{1,0:T(8,128)(2,1)} %bitcast.74, f32[64]{0:T(128)S(1)} %convolution_bitcast_fusion.5, f32[384,64]{0,1:T(8,128)S(1)} %convolution_bitcast_fusion.1), kind=kOutput, calls=%fused_computation.15 | convolution fusion | flops 403202048 | bytes 8487168 | tf_op jit(solution)/shard_map/dot_general | solution.py:79
  258.0 1.7 copy.11
  (50 shorter events, 14.8 us)
Async XLA Ops:
  7.2 185.6 %copy-start = (f32[384,64]{0,1:T(8,128)S(1)}, f32[384,64]{0,1:T(8,128)}, u32[]{:S(2)}) copy-start(f32[384,64]{0,1:T(8,128)} %param.6) | copy-start | bytes 294916
  7.2 185.6 %all-reduce.2.cloned.1.call-start = ((), (), s32[]{:S(2)}) async-start(), calls=%async_computation | async-start | bytes 1179648 | tf_op jit(solution)/shard_map/psum | solution.py:71
  8.3 9.1 %collective-permute-start = (bf16[2,128,384]{2,1,0:T(8,128)(2,1)S(1)}, bf16[2,128,384]{2,1,0:T(8,128)(2,1)S(1)}, u32[]{:S(2)}, u32[]{:S(2)}) collective-permute-start(bf16[2,128,384]{2,1,0:T(8,128)(2,1)S(1)} %get-tuple-element.10), channel_id=1, source_target_pairs={{0,4},{4,8},{8,12},{12,16},{16,20},{20,24},{24,28},{1,5},{5,9},{9,... | collective-permute-start | bytes 589832 | tf_op jit(solution)/shard_map/ppermute | solution.py:17
  13.2 8.8 %collective-permute-start.1 = (bf16[2,128,384]{2,1,0:T(8,128)(2,1)S(1)}, bf16[2,128,384]{2,1,0:T(8,128)(2,1)S(1)}, u32[]{:S(2)}, u32[]{:S(2)}) collective-permute-start(bf16[2,128,384]{2,1,0:T(8,128)(2,1)S(1)} %get-tuple-element.9), channel_id=1, source_target_pairs={{4,0},{8,4},{12,8},{16,12},{20,16},{24,20},{28,24},{5,1},{9,5},{13... | collective-permute-start | bytes 589832 | tf_op jit(solution)/shard_map/ppermute | solution.py:18
  22.2 2.7 %collective-permute-start.2 = (bf16[68,2,384]{2,1,0:T(2,128)(2,1)S(1)}, bf16[68,2,384]{2,1,0:T(2,128)(2,1)S(1)}, u32[]{:S(2)}, u32[]{:S(2)}) collective-permute-start(bf16[68,2,384]{2,1,0:T(2,128)(2,1)S(1)} %get-tuple-element.7), channel_id=1, source_target_pairs={{0,1},{1,2},{2,3},{4,5},{5,6},{6,7},{8,9},{9,10},{10,11},{12,13},{... | collective-permute-start | bytes 313352 | tf_op jit(solution)/shard_map/ppermute | solution.py:17
  23.5 5.0 %collective-permute-start.3 = (bf16[68,2,384]{2,1,0:T(2,128)(2,1)S(1)}, bf16[68,2,384]{2,1,0:T(2,128)(2,1)S(1)}, u32[]{:S(2)}, u32[]{:S(2)}) collective-permute-start(bf16[68,2,384]{2,1,0:T(2,128)(2,1)S(1)} %get-tuple-element.8), channel_id=1, source_target_pairs={{1,0},{2,1},{3,2},{5,4},{6,5},{7,6},{9,8},{10,9},{11,10},{13,12},{... | collective-permute-start | bytes 313352 | tf_op jit(solution)/shard_map/ppermute | solution.py:18
  104.5 155.2 %copy-start.1 = (f32[384]{0:T(512)}, f32[384]{0:T(512)S(1)}, u32[]{:S(2)}) copy-start(f32[384]{0:T(512)S(1)} %broadcast_multiply_fusion.1) | copy-start | bytes 4612
Sparse Core Ops, SparseCore 0:
  57.0 135.6 all-reduce.1
where the time goes:
time: 267 us
  waiting for transfers between devices  94.7 us (35%)
  other arithmetic  68 us (25%)
  blocking collectives  47.5 us (18%)
  matrix products  25.3 us (9%)
  between operations  14.4 us (5%)
  starting transfers between devices  8.8 us (3%)
  local copies, waits for them, and re-layouts  7.87 us (3%)
    psum x1, waiting for transfers between devices, local(): gram, sums = lax.psum((gram_local, sums_local), ('row', 'col'))  88.2 us
    psum x1, blocking collectives, local(): gram, sums = lax.psum((gram_local, sums_local), ('row', 'col'))  47.5 us
    another operation x12, other arithmetic, orthonormal(): lower_factor = jnp.linalg.cholesky(inner)  26.1 us
    another operation x8, other arithmetic, orthonormal(): lax.linalg.triangular_solve(lower_factor, product, left_side=False, lower...  22.2 us
    reduce_sum x1, other arithmetic, local(): sums_local = jnp.sum(flat, axis=0, dtype=jnp.float32)  9.75 us
    dot_general x1, matrix products, local(): lax.dot_general(flat, flat, (((0,), (0,)), ((), ())), preferred_element_t...  8.85 us
    dot_general x4, matrix products, local(): basis = orthonormal(jnp.dot(cov, basis, precision=lax.Precision.HIGHEST))  7.72 us
    unnamed x7, local copies, waits for them, and re-layouts  6.31 us
  transfers between devices with their start and end apart: 5, of which 3 were waited for; matrix products, arithmetic and copies ran while one was open for 2% of the time, Pallas kernels for 0%

commit v1 on v0

--- a/solution.py
+++ b/solution.py
@@ -68,7 +68,7 @@
     sums_local = jnp.sum(flat, axis=0, dtype=jnp.float32)
     count = float(rows_total * cols_total)
     basis = start
-    gram, sums = lax.psum((gram_local, sums_local), ("row", "col"))
+    gram, sums = lax.psum(lax.psum((gram_local, sums_local), "col"), "row")
     mean = sums / count
     cov = gram / count - mean[:, None] * mean[None, :]
     for step in range(ITERS):

time: 267 us -> 249 us (0.933)
  blocking collectives: 47.5 us -> 27.4 us
    psum x1 -> x2, blocking collectives: 47.5 us -> 27.4 us  [local(): gram, sums = lax.psum(lax.psum((gram_local, sums_local), 'col'), 'row')]
    psum x1 -> x2, waiting for transfers between devices: 88.2 us -> 90.6 us  [local(): gram, sums = lax.psum(lax.psum((gram_local, sums_local), 'col'), 'row')]
  transfers between devices with their start and end apart: 5 -> 6, of which waited for: 3 -> 4; matrix products, arithmetic and copies ran while one was open for 2% -> 2% of each run, Pallas kernels for 0% -> 0%
where the time goes in v1:
time: 249 us
  waiting for transfers between devices  97.1 us (39%)
  other arithmetic  68 us (27%)
  blocking collectives  27.4 us (11%)
  matrix products  25.3 us (10%)
  between operations  14.4 us (6%)
  starting transfers between devices  8.84 us (4%)
  local copies, waits for them, and re-layouts  7.87 us (3%)
    psum x2, waiting for transfers between devices, local(): gram, sums = lax.psum(lax.psum((gram_local, sums_local), 'col'), 'row')  90.6 us
    psum x2, blocking collectives, local(): gram, sums = lax.psum(lax.psum((gram_local, sums_local), 'col'), 'row')  27.4 us
    another operation x12, other arithmetic, orthonormal(): lower_factor = jnp.linalg.cholesky(inner)  26.1 us
    another operation x8, other arithmetic, orthonormal(): lax.linalg.triangular_solve(lower_factor, product, left_side=False, lower...  22.2 us
    reduce_sum x1, other arithmetic, local(): sums_local = jnp.sum(flat, axis=0, dtype=jnp.float32)  9.75 us
    dot_general x1, matrix products, local(): lax.dot_general(flat, flat, (((0,), (0,)), ((), ())), preferred_element_t...  8.85 us
    dot_general x4, matrix products, local(): basis = orthonormal(jnp.dot(cov, basis, precision=lax.Precision.HIGHEST))  7.72 us
    unnamed x7, local copies, waits for them, and re-layouts  6.31 us
  transfers between devices with their start and end apart: 6, of which 4 were waited for; matrix products, arithmetic and copies ran while one was open for 2% of the time, Pallas kernels for 0%

profile of v1, /device:TPU:0, one launch (start us, length us, event | category | flops | bytes accessed | tf_op | source)
XLA Modules:
  0.0 248.8 jit_solution(418254963578413365)
XLA Ops:
  8.3 4.9 %collective-permute-start = (bf16[2,128,384]{2,1,0:T(8,128)(2,1)S(1)}, bf16[2,128,384]{2,1,0:T(8,128)(2,1)S(1)}, u32[]{:S(2)}, u32[]{:S(2)}) collective-permute-start(bf16[2,128,384]{2,1,0:T(8,128)(2,1)S(1)} %get-tuple-element.10), channel_id=1, source_target_pairs={{0,4},{4,8},{8,12},{12,16},{16,20},{20,24},{24,28},{1,5},{5,9},{9,... | collective-permute-start | bytes 589832 | tf_op jit(solution)/shard_map/ppermute | solution.py:17
  14.5 2.9 %collective-permute-done = bf16[2,128,384]{2,1,0:T(8,128)(2,1)S(1)} collective-permute-done((bf16[2,128,384]{2,1,0:T(8,128)(2,1)S(1)}, bf16[2,128,384]{2,1,0:T(8,128)(2,1)S(1)}, u32[]{:S(2)}, u32[]{:S(2)}) %collective-permute-start) | collective-permute-done | bytes 196640 | tf_op jit(solution)/shard_map/ppermute | solution.py:17
  17.4 4.6 %constant_dynamic-update-slice_fusion.1 = bf16[68,128,384]{2,1,0:T(8,128)(2,1)S(1)} fusion(bf16[68,128,384]{2,1,0:T(8,128)(2,1)S(1)} %constant_dynamic-update-slice_fusion.2, bf16[64,128,384]{2,1,0:T(8,128)(2,1)} %param.5), kind=kLoop, calls=%fused_computation.56 | loop fusion | bytes 12582912
  24.9 3.6 %collective-permute-done.3 = bf16[68,2,384]{2,1,0:T(2,128)(2,1)S(1)} collective-permute-done((bf16[68,2,384]{2,1,0:T(2,128)(2,1)S(1)}, bf16[68,2,384]{2,1,0:T(2,128)(2,1)S(1)}, u32[]{:S(2)}, u32[]{:S(2)}) %collective-permute-start.3) | collective-permute-done | bytes 104480 | tf_op jit(solution)/shard_map/ppermute | solution.py:18
  28.5 3.6 %pad_maximum_fusion = bf16[68,132,384]{2,1,0:T(8,128)(2,1)S(1)} fusion(bf16[68,2,384]{2,1,0:T(2,128)(2,1)S(1)} %collective-permute-done.3, bf16[68,128,384]{2,1,0:T(8,128)(2,1)S(1)} %constant_dynamic-update-slice_fusion, bf16[68,2,384]{2,1,0:T(2,128)(2,1)S(1)} %collective-permute-done.2), kind=kLoop, calls=%fused_computation.14 | loop fusion | flops 20680704 | bytes 13787136 | tf_op jit(solution)/shard_map/concatenate | solution.py:19
  32.1 6.2 %multiply_add_fusion = f32[64,132,384]{2,1,0:T(8,128)S(1)} fusion(bf16[68,132,384]{2,1,0:T(8,128)(2,1)S(1)} %pad_maximum_fusion), kind=kLoop, calls=%fused_computation | loop fusion | flops 45416448 | bytes 45416448 | tf_op jit(solution)/shard_map/add | solution.py:35
  38.3 9.7 %convert_reduce_fusion = (f32[384]{0:T(512)S(1)}, bf16[64,128,384]{2,1,0:T(8,128)(2,1)}) fusion(f32[64,128]{1,0:T(8,128)S(1)} %broadcast_multiply_fusion, f32[64,132,384]{2,1,0:T(8,128)S(1)} %multiply_add_fusion), kind=kLoop, calls=%fused_computation.11 | loop fusion | flops 40894080 | bytes 69240320 | tf_op jit(solution)/shard_map/reduce_sum | solution.py:68
  48.1 8.8 %convolution_bitcast_fusion = f32[384,384]{1,0:T(8,128)} fusion(bf16[64,128,384]{2,1,0:T(8,128)(2,1)} %get-tuple-element.6), kind=kOutput, calls=%fused_computation.16 | convolution fusion | flops 2415919104 | bytes 6881280 | tf_op jit(solution)/shard_map/dot_general | solution.py:65
  57.0 41.2 %all-reduce.3.cloned.1.call-done = f32[384,384]{1,0:T(8,128)} async-done(((f32[384,384]{1,0:T(8,128)}), f32[384,384]{1,0:T(8,128)}) %all-reduce.3.cloned.1.call-update) | async-done | bytes 589840 | tf_op jit(solution)/shard_map/psum | solution.py:71
  98.2 5.8 %psum.28 = f32[384]{0:T(512)S(1)} all-reduce(f32[384]{0:T(512)S(1)} %get-tuple-element.5), channel_id=1, replica_groups=mesh['row'=8,'col'=4] {'col'}, use_global_device_ids=true, to_apply=%region_1.0 | all-reduce | flops 384 | bytes 3072 | tf_op jit(solution)/shard_map/psum | solution.py:71
  104.0 21.6 %psum.29 = f32[384]{0:T(512)S(1)} all-reduce(f32[384]{0:T(512)S(1)} %psum.28), channel_id=1, replica_groups=mesh['row'=8,'col'=4] {'row'}, use_global_device_ids=true, to_apply=%region_2.0 | all-reduce | flops 384 | bytes 3072 | tf_op jit(solution)/shard_map/psum | solution.py:71
  125.6 49.4 %all-reduce.5.cloned.1.call-done = f32[384,384]{1,0:T(8,128)} async-done(((f32[384,384]{1,0:T(8,128)}), f32[384,384]{1,0:T(8,128)}) %all-reduce.5.cloned.1.call-update) | async-done | bytes 589840 | tf_op jit(solution)/shard_map/psum | solution.py:71
  177.3 5.8 %cholesky.74 = f32[64,64]{1,0:T(8,128)S(1)} custom-call(f32[64,64]{1,0:T(8,128)S(1)} %fusion.18), custom_call_target="Cholesky" | custom-call | tf_op jit(solution)/shard_map/jit(cholesky)/cholesky | solution.py:48
  184.5 4.9 %custom-call.8 = f32[1,64,64]{1,2,0:T(8,128)S(1)} custom-call(f32[1,64,64]{2,1,0:T(8,128)S(1)} %fusion.7), custom_call_target="InvertDiagBlocksLowerTriangular" | custom-call | tf_op jit(solution)/shard_map/triangular_solve/custom-call.0 | solution.py:49
  189.7 1.9 fusion.37
  192.0 5.8 %cholesky.85 = f32[64,64]{1,0:T(8,128)S(1)} custom-call(f32[64,64]{1,0:T(8,128)S(1)} %fusion.16), custom_call_target="Cholesky" | custom-call | tf_op jit(solution)/shard_map/jit(cholesky)/cholesky | solution.py:48
  199.1 4.9 %custom-call.9 = f32[1,64,64]{1,2,0:T(8,128)S(1)} custom-call(f32[1,64,64]{2,1,0:T(8,128)S(1)} %fusion.8), custom_call_target="InvertDiagBlocksLowerTriangular" | custom-call | tf_op jit(solution)/shard_map/triangular_solve/custom-call.0 | solution.py:49
  204.3 1.9 fusion.36
  206.6 5.8 %cholesky.96 = f32[64,64]{1,0:T(8,128)S(1)} custom-call(f32[64,64]{1,0:T(8,128)S(1)} %fusion.14), custom_call_target="Cholesky" | custom-call | tf_op jit(solution)/shard_map/jit(cholesky)/cholesky | solution.py:48
  213.8 4.9 %custom-call.10 = f32[1,64,64]{1,2,0:T(8,128)S(1)} custom-call(f32[1,64,64]{2,1,0:T(8,128)S(1)} %fusion.9), custom_call_target="InvertDiagBlocksLowerTriangular" | custom-call | tf_op jit(solution)/shard_map/triangular_solve/custom-call.0 | solution.py:49
  219.0 1.9 fusion.35
  221.3 5.8 %cholesky.107 = f32[64,64]{1,0:T(8,128)S(1)} custom-call(f32[64,64]{1,0:T(8,128)S(1)} %fusion.12), custom_call_target="Cholesky" | custom-call | tf_op jit(solution)/shard_map/jit(cholesky)/cholesky | solution.py:48
  228.5 4.9 %custom-call.11 = f32[1,64,64]{1,2,0:T(8,128)S(1)} custom-call(f32[1,64,64]{2,1,0:T(8,128)S(1)} %fusion.10), custom_call_target="InvertDiagBlocksLowerTriangular" | custom-call | tf_op jit(solution)/shard_map/triangular_solve/custom-call.0 | solution.py:49
  235.3 4.9 %fusion.6 = f32[8,8,64,128]{3,1,2,0:T(8,128)S(1)} fusion(bf16[8192,384]{1,0:T(8,128)(2,1)} %bitcast.74, f32[64]{0:T(128)S(1)} %convolution_bitcast_fusion.5, f32[384,64]{0,1:T(8,128)S(1)} %convolution_bitcast_fusion.1), kind=kOutput, calls=%fused_computation.15 | convolution fusion | flops 403202048 | bytes 8487168 | tf_op jit(solution)/shard_map/dot_general | solution.py:79
  (54 shorter events, 18.5 us)
Async XLA Ops:
  7.2 167.8 %copy-start = (f32[384,64]{0,1:T(8,128)S(1)}, f32[384,64]{0,1:T(8,128)}, u32[]{:S(2)}) copy-start(f32[384,64]{0,1:T(8,128)} %param.6) | copy-start | bytes 294916
  7.2 91.0 %all-reduce.3.cloned.1.call-start = ((), (), s32[]{:S(2)}) async-start(), calls=%async_computation | async-start | bytes 1179648 | tf_op jit(solution)/shard_map/psum | solution.py:71
  8.3 9.1 %collective-permute-start = (bf16[2,128,384]{2,1,0:T(8,128)(2,1)S(1)}, bf16[2,128,384]{2,1,0:T(8,128)(2,1)S(1)}, u32[]{:S(2)}, u32[]{:S(2)}) collective-permute-start(bf16[2,128,384]{2,1,0:T(8,128)(2,1)S(1)} %get-tuple-element.10), channel_id=1, source_target_pairs={{0,4},{4,8},{8,12},{12,16},{16,20},{20,24},{24,28},{1,5},{5,9},{9,... | collective-permute-start | bytes 589832 | tf_op jit(solution)/shard_map/ppermute | solution.py:17
  13.2 8.8 %collective-permute-start.1 = (bf16[2,128,384]{2,1,0:T(8,128)(2,1)S(1)}, bf16[2,128,384]{2,1,0:T(8,128)(2,1)S(1)}, u32[]{:S(2)}, u32[]{:S(2)}) collective-permute-start(bf16[2,128,384]{2,1,0:T(8,128)(2,1)S(1)} %get-tuple-element.9), channel_id=1, source_target_pairs={{4,0},{8,4},{12,8},{16,12},{20,16},{24,20},{28,24},{5,1},{9,5},{13... | collective-permute-start | bytes 589832 | tf_op jit(solution)/shard_map/ppermute | solution.py:18
  22.2 2.7 %collective-permute-start.2 = (bf16[68,2,384]{2,1,0:T(2,128)(2,1)S(1)}, bf16[68,2,384]{2,1,0:T(2,128)(2,1)S(1)}, u32[]{:S(2)}, u32[]{:S(2)}) collective-permute-start(bf16[68,2,384]{2,1,0:T(2,128)(2,1)S(1)} %get-tuple-element.7), channel_id=1, source_target_pairs={{0,1},{1,2},{2,3},{4,5},{5,6},{6,7},{8,9},{9,10},{10,11},{12,13},{... | collective-permute-start | bytes 313352 | tf_op jit(solution)/shard_map/ppermute | solution.py:17
  23.5 5.0 %collective-permute-start.3 = (bf16[68,2,384]{2,1,0:T(2,128)(2,1)S(1)}, bf16[68,2,384]{2,1,0:T(2,128)(2,1)S(1)}, u32[]{:S(2)}, u32[]{:S(2)}) collective-permute-start(bf16[68,2,384]{2,1,0:T(2,128)(2,1)S(1)} %get-tuple-element.8), channel_id=1, source_target_pairs={{1,0},{2,1},{3,2},{5,4},{6,5},{7,6},{9,8},{10,9},{11,10},{13,12},{... | collective-permute-start | bytes 313352 | tf_op jit(solution)/shard_map/ppermute | solution.py:18
  56.9 118.1 %all-reduce.5.cloned.1.call-start = ((), (), s32[]{:S(2)}) async-start(), calls=%async_computation.1 | async-start | bytes 1179648 | tf_op jit(solution)/shard_map/psum | solution.py:71
  125.6 116.4 %copy-start.1 = (f32[384]{0:T(512)}, f32[384]{0:T(512)S(1)}, u32[]{:S(2)}) copy-start(f32[384]{0:T(512)S(1)} %broadcast_multiply_fusion.1) | copy-start | bytes 4612
Sparse Core Ops, SparseCore 0:
  57.0 41.0 all-reduce.2
  101.6 73.3 all-reduce.4
